TPU v7x, 32 devices: a whole 2x2x4 slice. The times are simulated.
32 devices in a mesh: layer: 4 (over x, core), feat: 4 (over z), par: 2 (over y).
Axes of the slice: x: 2, y: 2, z: 4, core: 2. Of those that a mesh axis runs over, the one named last changes fastest.
Arguments:
- residual: bfloat16 [4, 512, 2304], P('layer'), may hold values from -6 to 6
- norm_gain: float32 [4, 2304], P('layer'), may hold values from 0.5 to 1.5
- gate_weight: bfloat16 [4, 2304, 9216], P('layer', None, ('feat', 'par')), may hold values from -0.125 to 0.125
- up_weight: bfloat16 [4, 2304, 9216], P('layer', None, ('feat', 'par')), may hold values from -0.125 to 0.125
- down_weight: bfloat16 [4, 9216, 2304], P('layer', ('feat', 'par')), may hold values from -0.0625 to 0.0625
- enc_weight: float32 [4, 2304, 8192], P('layer', 'par', 'feat'), may hold values from -0.125 to 0.125
- enc_bias: float32 [4, 8192], P('layer', 'feat'), may hold values from -1 to 0.5
- dec_weight: bfloat16 [4, 2, 2, 8192, 2304], P('layer', 'par', None, 'feat'), may hold values from -0.0625 to 0.0625
- dec_bias: float32 [4, 2304], replicated, may hold values from -3 to 3
Outputs:
- enc_grad: float32 [4, 2304, 8192], P('layer', 'par', 'feat')
- enc_bias_grad: float32 [4, 8192], P('layer', 'feat')
- dec_grad: bfloat16 [4, 2, 2, 8192, 2304], P('layer', 'par', None, 'feat')
All inputs are finite; a program needn't handle non-finite values.
Results may differ from a plain program's by a relative error of at most 0.007.
Values may be sent and summed in bfloat16 or wider, within the bound.
No kernel may reach another device: no remote copies, remote signals or barrier semaphores. Data moves between devices by JAX's collectives and lax.ppermute only.
A program may use at most 192 MiB of HBM per device.

v0:
```python
import jax
import jax.numpy as jnp
from jax import lax
from jax.sharding import PartitionSpec as P


def partner_2(value, axis, stride):
    mask = 2**stride
    pairs = [(source, source ^ mask) for source in range(lax.axis_size(axis))]
    return lax.ppermute(value, axis, pairs)


def rms_normed(rows_in, gain_row):
    values = rows_in.astype(jnp.float32)
    scaling = lax.rsqrt(jnp.mean(values * values, axis=-1, keepdims=True) + 1e-06)
    return (values * scaling * gain_row).astype(jnp.bfloat16)


def shards(
    residual,
    norm_gain,
    gate_weight,
    up_weight,
    down_weight,
    enc_weight,
    enc_bias,
    dec_weight,
    dec_bias,
):
    highest = lax.Precision.HIGHEST
    source = lax.axis_index("layer")
    parity = lax.axis_index("par")
    slot_count = dec_weight.shape[2]
    normed = rms_normed(residual[0], norm_gain[0])
    tokens, model_width = normed.shape
    gate_value = jnp.dot(normed, gate_weight[0], preferred_element_type=jnp.float32)
    up_value = jnp.dot(normed, up_weight[0], preferred_element_type=jnp.float32)
    hidden = (jax.nn.gelu(gate_value, approximate=True) * up_value).astype(jnp.bfloat16)
    target_part = jnp.dot(hidden, down_weight[0], preferred_element_type=jnp.float32)
    half_width = enc_weight.shape[1]
    my_rows = lax.dynamic_slice_in_dim(normed, parity * half_width, half_width, 1).astype(
        jnp.float32
    )
    pre_part = jnp.dot(my_rows, enc_weight[0], precision=highest)
    pre_act = lax.psum(pre_part, "par") + enc_bias[0]
    positive = jnp.maximum(pre_act, 0.0)
    actives = (positive * positive).astype(jnp.bfloat16)
    slot_ids = jnp.arange(slot_count, dtype=jnp.int32)
    slot_live = 2 * slot_ids + parity >= source
    live_float = slot_live.astype(jnp.float32)
    decoders = dec_weight[0, 0]
    recon_parts = (
        jnp.einsum("tf,jfd->jtd", actives, decoders, preferred_element_type=jnp.float32)
        * live_float[:, None, None]
    )
    bias_slots = lax.dynamic_index_in_dim(
        dec_bias.reshape(slot_count, 2, model_width), parity, 1, keepdims=False
    )
    partner = partner_2(target_part, "par", 0)
    own_slot = ((slot_ids == source // 2) & (source % 2 == parity)).astype(jnp.float32)
    contrib = recon_parts - own_slot[:, None, None] * (target_part + partner)[None]
    summed_rows = lax.psum(contrib, ("layer", "feat"))
    err_full = summed_rows + bias_slots[:, None, :]
    errors = (err_full * 0.0625).astype(jnp.bfloat16)
    masked = errors * slot_live.astype(jnp.bfloat16)[:, None, None]
    back_part = jnp.einsum("jtd,jfd->tf", masked, decoders, preferred_element_type=jnp.float32)
    back_grad = lax.psum(back_part.astype(jnp.bfloat16), "par").astype(jnp.float32)
    d_pre = back_grad * 2.0 * positive
    enc_grad = lax.dot_general(my_rows, d_pre, (((0,), (0,)), ((), ())), precision=highest)
    bias_grad = jnp.sum(d_pre, axis=0)
    dec_grad = jnp.einsum(
        "tf,jtd->jfd", actives, masked, preferred_element_type=jnp.float32
    ).astype(jnp.bfloat16)
    return (enc_grad[None], bias_grad[None], dec_grad[None, None])


def solution(mesh):
    return jax.shard_map(
        shards,
        mesh=mesh,
        in_specs=(
            P("layer", None, None),
            P("layer", None),
            P("layer", None, ("feat", "par")),
            P("layer", None, ("feat", "par")),
            P("layer", ("feat", "par"), None),
            P("layer", "par", "feat"),
            P("layer", "feat"),
            P("layer", "par", None, "feat", None),
            P(),
        ),
        out_specs=(
            P("layer", "par", "feat"),
            P("layer", "feat"),
            P("layer", "par", None, "feat", None),
        ),
        check_vma=False,
    )
```

profile of v0, /device:TPU:0, one launch (start us, length us, event | category | flops | bytes accessed | tf_op | source)
XLA Modules:
  0.0 536.0 jit_solution(9293100787863199491)
XLA Ops:
  7.2 0.0 all-reduce.4.cloned.1.call-start
  7.2 2.2 multiply_reduce_fusion
  9.4 0.7 reduce
  10.2 0.0 copy-start
  10.2 8.3 %fusion.29 = f32[512,1152]{1,0:T(8,128)} fusion(bf16[1,2304,1152]{2,1,0:T(8,128)(2,1)} %param.11, bf16[1,512,2304]{2,1,0:T(8,128)(2,1)} %param.9, f32[2304]{0:T(1024)S(1)} %reduce, f32[512]{0:T(512)S(1)} %add_rsqrt_fusion), kind=kOutput, calls=%fused_computation.35 | convolution fusion | flops 2727346176 | bytes 10038272 | tf_op jit(solution)/shard_map/dot_general | solution.py:36
  18.4 0.0 copy-done
  18.4 13.4 %fusion.6 = f32[512,2304]{1,0:T(8,128)} fusion(bf16[1,1152,2304]{2,1,0:T(8,128)(2,1)} %param.13, f32[512,1152]{1,0:T(8,128)} %fusion.29, bf16[1,2304,1152]{2,1,0:T(8,128)(2,1)} %param.12, bf16[1,512,2304]{2,1,0:T(8,128)(2,1)S(1)} %copy-done, f32[2304]{0:T(1024)S(1)} %reduce, f32[512]{0:T(512)S(1)} %add_rsqrt_fusion), kind=kOutput, calls=%fused_computation.12 | convolution fusion | flops 5441716224 | bytes 20065280 | tf_op jit(solution)/shard_map/dot_general | solution.py:39
  31.8 3.0 collective-permute-start
  34.8 2.5 convert_bitcast_fusion.1
  37.3 0.1 dynamic-slice
  37.4 13.5 %fusion.4 = f32[512,2048]{1,0:T(8,128)} fusion(f32[1,1152,2048]{2,1,0:T(8,128)} %param.14, f32[512,2304]{1,0:T(8,128)} %convert_bitcast_fusion.1, s32[]{:T(128)S(6)} %select_n.18, f32[1152]{0:T(1024)S(1)} %dynamic-slice, f32[512]{0:T(512)S(1)} %add_rsqrt_fusion), kind=kOutput, calls=%fused_computation.6 | convolution fusion | flops 14497284096 | bytes 15997444 | tf_op jit(solution)/shard_map/dot_general | solution.py:44
  50.9 0.0 all-reduce.4.cloned.1.call-update
  50.9 0.0 all-reduce.6.cloned.1.call-start
  51.0 0.0 copy-start.4
  51.0 155.3 %collective-permute-done = f32[512,2304]{1,0:T(8,128)} collective-permute-done((f32[512,2304]{1,0:T(8,128)}, f32[512,2304]{1,0:T(8,128)}, u32[]{:S(2)}, u32[]{:S(2)}) %collective-permute-start) | collective-permute-done | bytes 4718624 | tf_op jit(solution)/shard_map/ppermute | solution.py:10
  206.3 6.5 %add.86 = f32[512,2304]{1,0:T(8,128)} add(f32[512,2304]{1,0:T(8,128)} %fusion.6, f32[512,2304]{1,0:T(8,128)} %collective-permute-done) | non-fusion elementwise | flops 1179648 | bytes 14155776 | tf_op jit(solution)/shard_map/add | solution.py:61
  212.8 14.1 %all-reduce.4.cloned.1.call-done = f32[512,2048]{1,0:T(8,128)} async-done(((f32[512,2048]{1,0:T(8,128)}), f32[512,2048]{1,0:T(8,128)}) %all-reduce.4.cloned.1.call-update) | async-done | bytes 4194320 | tf_op jit(solution)/shard_map/psum | solution.py:45
  226.9 0.0 copy-done.4
  226.9 18.0 %bitcast_subtract_fusion = f32[2,512,2304]{2,1,0:T(8,128)} fusion(f32[512,2304]{1,0:T(8,128)} %add.86, f32[2]{0:T(128)S(1)} %get-tuple-element.6, f32[2]{0:T(128)S(1)} %get-tuple-element.7, bf16[1,1,2,2048,2304]{4,3,2,1,0:T(8,128)(2,1)} %param.16, f32[512,2048]{1,0:T(8,128)} %all-reduce.4.cloned.1.call-done, f32[2048]{0:T(1024)S(1)} %bitcast.61), kind=kOutput, calls=%fused_computation.5 | convolution fusion | flops 9674948608 | bytes 37232656 | tf_op jit(solution)/shard_map/tf,jfd->jtd/dot_general | solution.py:53
  244.9 0.0 all-reduce.6.cloned.1.call-update
  245.0 0.0 all-reduce.8.cloned.1.call-start
  245.0 0.7 copy-done.3
  245.8 185.5 %all-reduce.6.cloned.1.call-done = f32[2,512,2304]{2,1,0:T(8,128)} async-done(((f32[2,512,2304]{2,1,0:T(8,128)}), f32[2,512,2304]{2,1,0:T(8,128)}) %all-reduce.6.cloned.1.call-update) | async-done | bytes 9437200 | tf_op jit(solution)/shard_map/psum | solution.py:62
  431.3 17.5 %bitcast_convert_fusion = bf16[512,2048]{1,0:T(8,128)(2,1)} fusion(bf16[1,1,2,2048,2304]{4,3,2,1,0:T(8,128)(2,1)} %param.16, f32[2,512,2304]{2,1,0:T(8,128)} %all-reduce.6.cloned.1.call-done, f32[2,2304]{1,0:T(2,128)S(1)} %bitcast.59, bf16[2]{0:T(256)(128)(2,1)S(1)} %compare_convert_fusion), kind=kOutput, calls=%fused_computation.22 | convolution fusion | flops 9674162176 | bytes 30427140 | tf_op jit(solution)/shard_map/jtd,jfd->tf/dot_general | solution.py:66
  448.8 0.0 all-reduce.8.cloned.1.call-update
  448.8 17.7 %convert_bitcast_fusion = bf16[1,1,2,2048,2304]{3,4,2,1,0:T(8,128)(2,1)} fusion(f32[512,2048]{1,0:T(8,128)} %all-reduce.4.cloned.1.call-done, f32[2048]{0:T(1024)S(1)} %bitcast.62, f32[2,512,2304]{2,1,0:T(8,128)} %all-reduce.6.cloned.1.call-done, f32[2,2304]{1,0:T(2,128)S(1)} %bitcast.60, bf16[2]{0:T(256)(128)(2,1)S(1)} %compare_convert_fusion), kind=kOutput, calls=%fused_computation.4 | convolution fusion | flops 9686745088 | bytes 32532484 | tf_op jit(solution)/shard_map/tf,jtd->jfd/dot_general | solution.py:71
  466.5 24.8 %copy.13 = bf16[1,1,2,2048,2304]{4,3,2,1,0:T(8,128)(2,1)} copy(bf16[1,1,2,2048,2304]{3,4,2,1,0:T(8,128)(2,1)} %convert_bitcast_fusion) | data formatting | bytes 37748736
  491.2 20.8 %all-reduce.8.cloned.1.call-done = bf16[512,2048]{1,0:T(8,128)(2,1)} async-done(((bf16[512,2048]{1,0:T(8,128)(2,1)}), bf16[512,2048]{1,0:T(8,128)(2,1)}) %all-reduce.8.cloned.1.call-update) | async-done | bytes 2097168 | tf_op jit(solution)/shard_map/psum | solution.py:67
  512.0 4.5 fusion.35
  516.5 0.0 copy-done.1
  516.5 0.3 copy-done.2
  516.7 12.7 %convolution_bitcast_fusion = f32[1,1152,2048]{2,1,0:T(8,128)} fusion(bf16[512,2048]{1,0:T(8,128)(2,1)S(1)} %copy-done.2, f32[512,2048]{1,0:T(8,128)S(1)} %copy-done.1, f32[2048]{0:T(1024)S(1)} %bitcast.64, f32[512,2304]{1,0:T(8,128)} %convert_bitcast_fusion.1, s32[]{:T(128)S(6)} %select_n.18, f32[1152]{0:T(1024)S(1)} %dynamic-slice, f32[512]{0:T(512)S(1)} %add_rsqrt_fusion), kind=kOutput, calls=%fused_computation.9 | convolution fusion | flops 14502526976 | bytes 18102788 | tf_op jit(solution)/shard_map/dot_general | solution.py:69
  (9 shorter events, 0.1 us)
Async XLA Ops:
  7.2 219.8 %all-reduce.4.cloned.1.call-start = ((), (), s32[]{:S(2)}) async-start(), calls=%async_computation | async-start | bytes 8388608 | tf_op jit(solution)/shard_map/psum | solution.py:45
  10.2 8.3 %copy-start = (bf16[1,512,2304]{2,1,0:T(8,128)(2,1)S(1)}, bf16[1,512,2304]{2,1,0:T(8,128)(2,1)}, u32[]{:S(2)}) copy-start(bf16[1,512,2304]{2,1,0:T(8,128)(2,1)} %param.9) | copy-start | bytes 7077892
  31.8 174.5 %collective-permute-start = (f32[512,2304]{1,0:T(8,128)}, f32[512,2304]{1,0:T(8,128)}, u32[]{:S(2)}, u32[]{:S(2)}) collective-permute-start(f32[512,2304]{1,0:T(8,128)} %fusion.6), channel_id=1, source_target_pairs={{0,1},{1,0},{2,3},{3,2},{4,5},{5,4},{6,7},{7,6},{8,9},{9,8},{10,11... | collective-permute-start | bytes 14155784 | tf_op jit(solution)/shard_map/ppermute | solution.py:10
  50.9 380.4 %all-reduce.6.cloned.1.call-start = ((), (), s32[]{:S(2)}) async-start(), calls=%async_computation.1 | async-start | bytes 18874368 | tf_op jit(solution)/shard_map/psum | solution.py:62
  51.0 176.0 %copy-start.4 = (f32[1,2048]{1,0:T(1,128)S(1)}, f32[1,2048]{1,0:T(1,128)}, u32[]{:S(2)}) copy-start(f32[1,2048]{1,0:T(1,128)} %param.15) | copy-start | bytes 24580
  244.9 0.8 copy-start.3
  245.0 267.1 %all-reduce.8.cloned.1.call-start = ((), (), s32[]{:S(2)}) async-start(), calls=%async_computation.2 | async-start | bytes 4194304 | tf_op jit(solution)/shard_map/psum | solution.py:67
  512.0 4.5 copy-start.1
  512.0 4.7 copy-start.2
Sparse Core Ops, SparseCore 0:
  51.0 175.8 all-reduce.3
  245.1 186.1 all-reduce.5
  448.9 63.0 all-reduce.7
where the time goes:
time: 537 us; the launch traced here: 536 us
  waiting for transfers between devices  376 us (70%)
  matrix products  101 us (19%)
  local copies, waits for them, and re-layouts  25.9 us (5%)
  other arithmetic  16.4 us (3%)
  between operations  13.8 us (3%)
    psum x1, waiting for transfers between devices, shards(): summed_rows = lax.psum(contrib, ('layer', 'feat'))  185 us
    ppermute x1, waiting for transfers between devices, partner_2(): return lax.ppermute(value, axis, pairs)  155 us
    unnamed x12, local copies, waits for them, and re-layouts  25.8 us
    psum x1, waiting for transfers between devices, shards(): lax.psum(back_part.astype(jnp.bfloat16), 'par').astype(jnp.float32)  20.8 us
    dot_general x1, matrix products, shards(): jnp.einsum('tf,jfd->jtd', actives, decoders, preferred_element_type=jnp.f...  18 us
    dot_general x1, matrix products, shards(): jnp.einsum('tf,jtd->jfd', actives, masked, preferred_element_type=jnp.flo...  17.7 us
    dot_general x1, matrix products, shards(): jnp.einsum('jtd,jfd->tf', masked, decoders, preferred_element_type=jnp.fl...  17.5 us
    psum x1, waiting for transfers between devices, shards(): pre_act = lax.psum(pre_part, 'par') + enc_bias[0]  14.1 us
  transfers between devices with their start and end apart: 4, of which 4 were waited for; matrix products, arithmetic and copies ran while one was open for 12% of the time, Pallas kernels for 0%

commit v1 on v0

--- a/solution.py
+++ b/solution.py
@@ -59,7 +59,7 @@
     partner = partner_2(target_part, "par", 0)
     own_slot = ((slot_ids == source // 2) & (source % 2 == parity)).astype(jnp.float32)
     contrib = recon_parts - own_slot[:, None, None] * (target_part + partner)[None]
-    summed_rows = lax.psum(contrib, ("layer", "feat"))
+    summed_rows = lax.psum(lax.psum(contrib, "feat"), "layer")
     err_full = summed_rows + bias_slots[:, None, :]
     errors = (err_full * 0.0625).astype(jnp.bfloat16)
     masked = errors * slot_live.astype(jnp.bfloat16)[:, None, None]

time: 537 us -> 848 us (1.58)
  waiting for transfers between devices: 376 us -> 687 us
    psum x1 -> x2, waiting for transfers between devices: 185 us -> 497 us  [shards(): summed_rows = lax.psum(lax.psum(contrib, 'feat'), 'layer')]
  transfers between devices with their start and end apart: 4 -> 5, of which waited for: 4 -> 5; matrix products, arithmetic and copies ran while one was open for 12% -> 8% of each run, Pallas kernels for 0% -> 0%
where the time goes in v1:
time: 848 us; the launch traced here: 847 us
  waiting for transfers between devices  687 us (81%)
  matrix products  101 us (12%)
  local copies, waits for them, and re-layouts  25.9 us (3%)
  other arithmetic  16.4 us (2%)
  between operations  13.8 us (2%)
    psum x2, waiting for transfers between devices, shards(): summed_rows = lax.psum(lax.psum(contrib, 'feat'), 'layer')  497 us
    ppermute x1, waiting for transfers between devices, partner_2(): return lax.ppermute(value, axis, pairs)  155 us
    unnamed x12, local copies, waits for them, and re-layouts  25.8 us
    psum x1, waiting for transfers between devices, shards(): lax.psum(back_part.astype(jnp.bfloat16), 'par').astype(jnp.float32)  20.9 us
    dot_general x1, matrix products, shards(): jnp.einsum('tf,jfd->jtd', actives, decoders, preferred_element_type=jnp.f...  18 us
    dot_general x1, matrix products, shards(): jnp.einsum('tf,jtd->jfd', actives, masked, preferred_element_type=jnp.flo...  17.7 us
    dot_general x1, matrix products, shards(): jnp.einsum('jtd,jfd->tf', masked, decoders, preferred_element_type=jnp.fl...  17.5 us
  transfers between devices with their start and end apart: 5, of which 5 were waited for; matrix products, arithmetic and copies ran while one was open for 8% of the time, Pallas kernels for 0%

profile of v1, /device:TPU:0, one launch (start us, length us, event | category | flops | bytes accessed | tf_op | source)
XLA Modules:
  0.0 847.4 jit_solution(15310483714877353855)
XLA Ops:
  7.2 0.0 all-reduce.5.cloned.1.call-start
  7.2 2.2 multiply_reduce_fusion
  9.4 0.7 reduce
  10.2 0.0 copy-start
  10.2 8.3 fusion.29
  18.4 13.4 %fusion.6 = f32[512,2304]{1,0:T(8,128)} fusion(bf16[1,1152,2304]{2,1,0:T(8,128)(2,1)} %param.13, f32[512,1152]{1,0:T(8,128)} %fusion.29, bf16[1,2304,1152]{2,1,0:T(8,128)(2,1)} %param.12, bf16[1,512,2304]{2,1,0:T(8,128)(2,1)S(1)} %copy-done, f32[2304]{0:T(1024)S(1)} %reduce, f32[512]{0:T(512)S(1)} %add_rsqrt_fusion), kind=kOutput, calls=%fused_computation.12 | convolution fusion | flops 5441716224 | bytes 20065280 | tf_op jit(solution)/shard_map/dot_general | solution.py:39
  31.8 3.0 collective-permute-start
  34.8 2.5 convert_bitcast_fusion.1
  37.3 0.1 dynamic-slice
  37.4 13.5 %fusion.4 = f32[512,2048]{1,0:T(8,128)} fusion(f32[1,1152,2048]{2,1,0:T(8,128)} %param.14, f32[512,2304]{1,0:T(8,128)} %convert_bitcast_fusion.1, s32[]{:T(128)S(6)} %select_n.18, f32[1152]{0:T(1024)S(1)} %dynamic-slice, f32[512]{0:T(512)S(1)} %add_rsqrt_fusion), kind=kOutput, calls=%fused_computation.6 | convolution fusion | flops 14497284096 | bytes 15997444 | tf_op jit(solution)/shard_map/dot_general | solution.py:44
  50.9 0.0 all-reduce.5.cloned.1.call-update
  50.9 0.0 all-reduce.7.cloned.1.call-start
  51.0 0.0 copy-start.4
  51.0 155.3 %collective-permute-done = f32[512,2304]{1,0:T(8,128)} collective-permute-done((f32[512,2304]{1,0:T(8,128)}, f32[512,2304]{1,0:T(8,128)}, u32[]{:S(2)}, u32[]{:S(2)}) %collective-permute-start) | collective-permute-done | bytes 4718624 | tf_op jit(solution)/shard_map/ppermute | solution.py:10
  206.3 6.5 add.88
  212.8 14.1 %all-reduce.5.cloned.1.call-done = f32[512,2048]{1,0:T(8,128)} async-done(((f32[512,2048]{1,0:T(8,128)}), f32[512,2048]{1,0:T(8,128)}) %all-reduce.5.cloned.1.call-update) | async-done | bytes 4194320 | tf_op jit(solution)/shard_map/psum | solution.py:45
  226.9 18.0 %bitcast_subtract_fusion = f32[2,512,2304]{2,1,0:T(8,128)} fusion(f32[512,2304]{1,0:T(8,128)} %add.88, f32[2]{0:T(128)S(1)} %get-tuple-element.6, f32[2]{0:T(128)S(1)} %get-tuple-element.7, bf16[1,1,2,2048,2304]{4,3,2,1,0:T(8,128)(2,1)} %param.16, f32[512,2048]{1,0:T(8,128)} %all-reduce.5.cloned.1.call-done, f32[2048]{0:T(1024)S(1)} %bitcast.61), kind=kOutput, calls=%fused_computation.5 | convolution fusion | flops 9674948608 | bytes 37232656 | tf_op jit(solution)/shard_map/tf,jfd->jtd/dot_general | solution.py:53
  244.9 0.0 all-reduce.7.cloned.1.call-update
  245.0 0.0 all-reduce.9.cloned.1.call-start
  245.0 326.2 %all-reduce.7.cloned.1.call-done = f32[2,512,2304]{2,1,0:T(8,128)} async-done(((f32[2,512,2304]{2,1,0:T(8,128)}), f32[2,512,2304]{2,1,0:T(8,128)}) %all-reduce.7.cloned.1.call-update) | async-done | bytes 9437200 | tf_op jit(solution)/shard_map/psum | solution.py:62
  571.2 0.0 all-reduce.9.cloned.1.call-update
  571.3 0.0 all-reduce.11.cloned.1.call-start
  571.3 0.7 copy-done.3
  572.1 170.4 %all-reduce.9.cloned.1.call-done = f32[2,512,2304]{2,1,0:T(8,128)} async-done(((f32[2,512,2304]{2,1,0:T(8,128)}), f32[2,512,2304]{2,1,0:T(8,128)}) %all-reduce.9.cloned.1.call-update) | async-done | bytes 9437200 | tf_op jit(solution)/shard_map/psum | solution.py:62
  742.5 17.5 %bitcast_convert_fusion = bf16[512,2048]{1,0:T(8,128)(2,1)} fusion(bf16[1,1,2,2048,2304]{4,3,2,1,0:T(8,128)(2,1)} %param.16, f32[2,512,2304]{2,1,0:T(8,128)} %all-reduce.9.cloned.1.call-done, f32[2,2304]{1,0:T(2,128)S(1)} %bitcast.59, bf16[2]{0:T(256)(128)(2,1)S(1)} %compare_convert_fusion), kind=kOutput, calls=%fused_computation.22 | convolution fusion | flops 9674162176 | bytes 30427140 | tf_op jit(solution)/shard_map/jtd,jfd->tf/dot_general | solution.py:66
  760.0 0.0 all-reduce.11.cloned.1.call-update
  760.1 17.7 %convert_bitcast_fusion = bf16[1,1,2,2048,2304]{3,4,2,1,0:T(8,128)(2,1)} fusion(f32[512,2048]{1,0:T(8,128)} %all-reduce.5.cloned.1.call-done, f32[2048]{0:T(1024)S(1)} %bitcast.62, f32[2,512,2304]{2,1,0:T(8,128)} %all-reduce.9.cloned.1.call-done, f32[2,2304]{1,0:T(2,128)S(1)} %bitcast.60, bf16[2]{0:T(256)(128)(2,1)S(1)} %compare_convert_fusion), kind=kOutput, calls=%fused_computation.4 | convolution fusion | flops 9686745088 | bytes 32532484 | tf_op jit(solution)/shard_map/tf,jtd->jfd/dot_general | solution.py:71
  777.7 24.8 %copy.13 = bf16[1,1,2,2048,2304]{4,3,2,1,0:T(8,128)(2,1)} copy(bf16[1,1,2,2048,2304]{3,4,2,1,0:T(8,128)(2,1)} %convert_bitcast_fusion) | data formatting | bytes 37748736
  802.5 20.9 %all-reduce.11.cloned.1.call-done = bf16[512,2048]{1,0:T(8,128)(2,1)} async-done(((bf16[512,2048]{1,0:T(8,128)(2,1)}), bf16[512,2048]{1,0:T(8,128)(2,1)}) %all-reduce.11.cloned.1.call-update) | async-done | bytes 2097168 | tf_op jit(solution)/shard_map/psum | solution.py:67
  823.4 4.5 fusion.35
  827.8 0.3 copy-done.2
  828.1 12.7 %convolution_bitcast_fusion = f32[1,1152,2048]{2,1,0:T(8,128)} fusion(bf16[512,2048]{1,0:T(8,128)(2,1)S(1)} %copy-done.2, f32[512,2048]{1,0:T(8,128)S(1)} %copy-done.1, f32[2048]{0:T(1024)S(1)} %bitcast.64, f32[512,2304]{1,0:T(8,128)} %convert_bitcast_fusion.1, s32[]{:T(128)S(6)} %select_n.18, f32[1152]{0:T(1024)S(1)} %dynamic-slice, f32[512]{0:T(512)S(1)} %add_rsqrt_fusion), kind=kOutput, calls=%fused_computation.9 | convolution fusion | flops 14502526976 | bytes 18102788 | tf_op jit(solution)/shard_map/dot_general | solution.py:69
  (12 shorter events, 0.1 us)
Async XLA Ops:
  7.2 219.8 %all-reduce.5.cloned.1.call-start = ((), (), s32[]{:S(2)}) async-start(), calls=%async_computation | async-start | bytes 8388608 | tf_op jit(solution)/shard_map/psum | solution.py:45
  10.2 8.3 copy-start
  31.8 174.5 %collective-permute-start = (f32[512,2304]{1,0:T(8,128)}, f32[512,2304]{1,0:T(8,128)}, u32[]{:S(2)}, u32[]{:S(2)}) collective-permute-start(f32[512,2304]{1,0:T(8,128)} %fusion.6), channel_id=1, source_target_pairs={{0,1},{1,0},{2,3},{3,2},{4,5},{5,4},{6,7},{7,6},{8,9},{9,8},{10,11... | collective-permute-start | bytes 14155784 | tf_op jit(solution)/shard_map/ppermute | solution.py:10
  50.9 520.4 %all-reduce.7.cloned.1.call-start = ((), (), s32[]{:S(2)}) async-start(), calls=%async_computation.1 | async-start | bytes 18874368 | tf_op jit(solution)/shard_map/psum | solution.py:62
  51.0 176.0 %copy-start.4 = (f32[1,2048]{1,0:T(1,128)S(1)}, f32[1,2048]{1,0:T(1,128)}, u32[]{:S(2)}) copy-start(f32[1,2048]{1,0:T(1,128)} %param.15) | copy-start | bytes 24580
  245.0 497.6 %all-reduce.9.cloned.1.call-start = ((), (), s32[]{:S(2)}) async-start(), calls=%async_computation.2 | async-start | bytes 18874368 | tf_op jit(solution)/shard_map/psum | solution.py:62
  571.2 0.8 copy-start.3
  571.3 252.1 %all-reduce.11.cloned.1.call-start = ((), (), s32[]{:S(2)}) async-start(), calls=%async_computation.3 | async-start | bytes 4194304 | tf_op jit(solution)/shard_map/psum | solution.py:67
  823.4 4.5 copy-start.1
  823.4 4.7 copy-start.2
Sparse Core Ops, SparseCore 0:
  51.0 175.8 all-reduce.4
  245.1 326.1 all-reduce.6
  573.7 168.7 all-reduce.8
  760.2 63.1 all-reduce.10
